TPU v7x, 512 devices: a whole 4x8x8 slice. The times are simulated.
512 devices in a mesh: gx: 16 (over y_hi, x, core), gy: 4 (over y_lo), gz: 8 (over z).
Axes of the slice: x: 4, y: 8 (y_hi: 2, y_lo: 4; y = y_hi * 4 + y_lo), z: 8, core: 2. Of those that a mesh axis runs over, the one named last changes fastest.
Arguments:
- velocity: float32 [3, 32, 4, 32, 512], P(None, 'gx', 'gy', 'gz'), may hold values from -4 to 4
- reaction: float32 [32, 4, 32, 512], P('gx', 'gy', 'gz'), may hold values from 10 to 100
Outputs:
- velocity_out: float32 [3, 32, 4, 32, 512], P(None, 'gx', 'gy', 'gz')
- pressure: float32 [32, 4, 32, 512], P('gx', 'gy', 'gz')
- residual: float32 [32, 4, 32, 512], P('gx', 'gy', 'gz')
All inputs are finite; a program needn't handle non-finite values.
Results may differ from a plain program's by a relative error of at most 0.007.
Values sent between devices are 32-bit elements; how exact they have to be, the bound alone decides.
A program may use at most 64 MiB of HBM per device.

v0:
```python
import jax
import jax.numpy as jnp
import numpy as np
from jax import lax
from jax.sharding import PartitionSpec as P

SUBSTEPS = 2
ITERS = 4
step_size = 0.02


def extended(block, sides, width, periodic):
    for axis, dim in sides:
        count = lax.axis_size(axis)
        forward = [(i, i + 1) for i in range(count - 1)]
        if periodic:
            forward.append((count - 1, 0))
        backward = [(target, source) for source, target in forward]
        low = lax.ppermute(
            lax.slice_in_dim(block, block.shape[dim] - width, None, axis=dim), axis, forward
        )
        high = lax.ppermute(lax.slice_in_dim(block, 0, width, axis=dim), axis, backward)
        block = jnp.concatenate([low, block, high], axis=dim)
    return block


def legendre_seven(points):
    earlier = points * 0.0 + 1.0
    current = points
    for degree in range(1, 7):
        earlier, current = (
            current,
            ((2 * degree + 1) * points * current - degree * earlier) / (degree + 1),
        )
    return current


def tables():
    half = np.array([0.20929921790247888, 0.5917001814331423, 0.8717401485096066, 1.0])
    points = np.concatenate([-half[::-1], half])
    legendre = legendre_seven(points)
    weights = 2.0 / (56.0 * legendre**2)
    spacing = points[:, None] - points[None, :] + np.eye(8)
    derivative = legendre[:, None] / legendre[None, :] / spacing * (1.0 - np.eye(8))
    derivative[0, 0] = -14.0
    derivative[7, 7] = 14.0
    return (jnp.asarray(weights, jnp.float32), jnp.asarray(derivative, jnp.float32))


def derive(values, derivative, along_dim, transposed):
    layout = values.shape
    matrix = derivative.T if transposed else derivative
    blocks = values.reshape(-1, 8, 8, 8)
    patterns = ("aq,nqbc->nabc", "bq,naqc->nabc", "cq,nabq->nabc")
    result = jnp.einsum(patterns[along_dim], matrix, blocks, precision=lax.Precision.HIGHEST)
    return result.reshape(layout)


def place_face(values, target_axis, position, update):
    selector = tuple(
        (position if place == target_axis else slice(None) for place in range(values.ndim))
    )
    return values.at[selector].set(update)


def faces_along_x(sequence):
    return extended(sequence, (("gx", 0),), 1, True)


def faces_along_y(sequence):
    return extended(sequence, (("gy", 0),), 1, False)


def faces_along_z(sequence):
    return extended(sequence, (("gz", 0),), 1, False)


def join_faces(values, along_dim, exchanger):
    lower_face = jnp.moveaxis(jnp.take(values, 0, axis=4 + along_dim), 1 + along_dim, 0)
    upper_face = jnp.moveaxis(jnp.take(values, 7, axis=4 + along_dim), 1 + along_dim, 0)
    elements = lower_face.shape[0]
    face_shape = lower_face.shape
    sequence = jnp.stack([lower_face, upper_face], axis=1).reshape(2 * elements, -1)
    padded = exchanger(sequence)
    paired = padded.reshape(elements + 1, 2, -1)
    totals = paired[:, 0] + paired[:, 1]
    new_lower = jnp.moveaxis(totals[:-1].reshape(face_shape), 0, 1 + along_dim)
    new_upper = jnp.moveaxis(totals[1:].reshape(face_shape), 0, 1 + along_dim)
    values = place_face(values, 4 + along_dim, 0, new_lower)
    return place_face(values, 4 + along_dim, 7, new_upper)


def assemble(values):
    exchangers = (faces_along_x, faces_along_y, faces_along_z)
    dim_order = (0, 1, 2)
    for along_dim in dim_order:
        values = join_faces(values, along_dim, exchangers[along_dim])
    return values


def dim_factors(local_count, offset, total_count, bounded_by_walls):
    element_ids = offset + jnp.arange(local_count)
    node_ids = jnp.arange(8)
    at_end = (node_ids[None, :] == 0) | (node_ids[None, :] == 7)
    low_wall = (element_ids[:, None] == 0) & (node_ids[None, :] == 0)
    high_wall = (element_ids[:, None] == total_count - 1) & (node_ids[None, :] == 7)
    on_wall = (low_wall | high_wall) & bounded_by_walls
    shared = at_end & jnp.logical_not(on_wall)
    return (jnp.where(shared, 2.0, 1.0).astype(jnp.float32), on_wall.astype(jnp.float32))


def body(velocity, reaction):
    weights, derivative = tables()
    count_x, count_y, count_z = (reaction.shape[0], reaction.shape[1], reaction.shape[2])
    speed = velocity.reshape(3, count_x, count_y, count_z, 8, 8, 8)
    react = reaction.reshape(1, count_x, count_y, count_z, 8, 8, 8)
    mass_matrix = weights[:, None, None] * weights[None, :, None] * weights[None, None, :]
    factor_x, wall_x = dim_factors(
        count_x, lax.axis_index("gx") * count_x, lax.axis_size("gx") * count_x, False
    )
    factor_y, wall_y = dim_factors(
        count_y, lax.axis_index("gy") * count_y, lax.axis_size("gy") * count_y, True
    )
    factor_z, wall_z = dim_factors(
        count_z, lax.axis_index("gz") * count_z, lax.axis_size("gz") * count_z, True
    )
    multiplicity = (
        factor_x[None, :, None, None, :, None, None]
        * factor_y[None, None, :, None, None, :, None]
        * factor_z[None, None, None, :, None, None, :]
    )
    interior = (1.0 - wall_y[None, None, :, None, None, :, None]) * (
        1.0 - wall_z[None, None, None, :, None, None, :]
    )
    stiff_sum = jnp.sum(weights[:, None] * derivative * derivative, axis=0)
    diag_local = (
        stiff_sum[:, None, None] * weights[None, :, None] * weights[None, None, :]
        + weights[:, None, None] * stiff_sum[None, :, None] * weights[None, None, :]
        + weights[:, None, None] * weights[None, :, None] * stiff_sum[None, None, :]
    )
    diag_terms = diag_local + react * mass_matrix
    speed = assemble(speed) / multiplicity
    diagonal = None
    for substep in range(SUBSTEPS):
        gradient_fields = [derive(speed, derivative, along_dim, False) for along_dim in range(3)]
        transport = (
            speed[0:1] * gradient_fields[0]
            + speed[1:2] * gradient_fields[1]
            + speed[2:3] * gradient_fields[2]
        )
        tendency = assemble(mass_matrix * transport) / (mass_matrix * multiplicity)
        speed = interior * (speed - step_size * tendency)
    spread = (
        derive(speed[0:1], derivative, 0, False)
        + derive(speed[1:2], derivative, 1, False)
        + derive(speed[2:3], derivative, 2, False)
    )
    source = -assemble(mass_matrix * spread)
    diagonal = assemble(diag_terms)

    def local_inner(first, second):
        return jnp.sum(first * second / multiplicity)

    def norm_weighted_mass(residual_vec, precond_vec):
        return lax.psum(local_inner(residual_vec, precond_vec), ("gx", "gy", "gz"))

    pressure = jnp.zeros_like(source)
    residual = source
    precond = residual / diagonal
    search = precond
    progress = norm_weighted_mass(residual, precond)
    for sweep_index in range(ITERS):
        local_sum = react * mass_matrix * search
        for apply_along_dim in range(3):
            local_sum = local_sum + derive(
                mass_matrix * derive(search, derivative, apply_along_dim, False),
                derivative,
                apply_along_dim,
                True,
            )
        applied = assemble(local_sum)
        step_length = progress / lax.psum(local_inner(search, applied), ("gx", "gy", "gz"))
        pressure = pressure + step_length * search
        residual = residual - step_length * applied
        precond = residual / diagonal
        progress_next = norm_weighted_mass(residual, precond)
        search = precond + progress_next / progress * search
        progress = progress_next
    return (
        speed.reshape(3, count_x, count_y, count_z, 512),
        pressure.reshape(count_x, count_y, count_z, 512),
        residual.reshape(count_x, count_y, count_z, 512),
    )


def solution(mesh):
    in_specs = (P(None, "gx", "gy", "gz", None), P("gx", "gy", "gz", None))
    out_specs = (
        P(None, "gx", "gy", "gz", None),
        P("gx", "gy", "gz", None),
        P("gx", "gy", "gz", None),
    )
    return jax.shard_map(body, mesh=mesh, in_specs=in_specs, out_specs=out_specs, check_vma=False)
```

profile of v0, /device:TPU:1, one launch (start us, length us, event | category | flops | bytes accessed | tf_op | source)
XLA Modules:
  0.0 1127.1 jit_solution(3727668878768256225)
XLA Ops:
  2.1 4.5 collective-permute-start
  6.6 6.2 collective-permute-start.1
  15.8 9.7 collective-permute-start.25
  30.0 4.0 collective-permute-start.2
  35.4 3.0 collective-permute-done.3
  46.6 3.0 collective-permute-done.5
  51.0 2.6 scatter.186
  54.8 15.4 %scatter.189 = f32[3,2,1,4,8,8,8]{6,5,4,3,1,0,2:T(8,128)S(1)} dynamic-update-slice(f32[3,2,1,4,8,8,8]{6,5,4,3,1,0,2:T(8,128)S(1)} %scatter.186, f32[3,2,1,4,8,8,1]{6,5,4,3,1,0,2:T(8,128)S(1)} %copy.186, s32[]{:T(128)} %constant.1319.clone.1, s32[]{:T(128)} %constant.1319.clone.1, s32[]{:T(128)} %constant.1319.clone.1, s32[]{:T(128)} %constant.1319.clone.1, s32[]{:T(128)} %constant.1319.clone.1, ...) | dynamic-update-slice | bytes 12292 | tf_op jit(solution)/shard_map/scatter | solution.py:63
  76.7 2.4 fusion.2
  79.4 2.2 collective-permute-start.6
  81.6 12.9 %collective-permute-start.7 = (f32[1,768]{1,0:T(1,128)S(1)}, f32[1,768]{1,0:T(1,128)S(1)}, u32[]{:S(2)}, u32[]{:S(2)}) collective-permute-start(f32[1,768]{1,0:T(1,128)S(1)} %get-tuple-element.938), channel_id=1, source_target_pairs={{32,0},{64,32},{96,64},{128,96},{160,128},{192,160},{224,192},{256... | collective-permute-start | bytes 9224 | tf_op jit(solution)/shard_map/ppermute | solution.py:22
  95.9 3.2 collective-permute-start.8
  100.8 2.8 collective-permute-done.9
  109.1 4.0 collective-permute-start.10
  114.5 4.7 collective-permute-done.11
  120.1 2.1 copy.201
  122.1 2.6 scatter.196
  127.5 15.4 %scatter.199 = f32[3,2,1,4,8,8,8]{6,5,4,3,1,0,2:T(8,128)S(1)} dynamic-update-slice(f32[3,2,1,4,8,8,8]{6,5,4,3,1,0,2:T(8,128)S(1)} %scatter.196, f32[3,2,1,4,8,8,1]{6,5,4,3,1,0,2:T(8,128)S(1)} %copy.203, s32[]{:T(128)} %constant.1319.clone.1, s32[]{:T(128)} %constant.1319.clone.1, s32[]{:T(128)} %constant.1319.clone.1, s32[]{:T(128)} %constant.1319.clone.1, s32[]{:T(128)} %constant.1319.clone.1, ...) | dynamic-update-slice | bytes 12292 | tf_op jit(solution)/shard_map/scatter | solution.py:63
  148.1 2.2 fusion.5
  152.4 12.7 %collective-permute-start.13 = (f32[1,768]{1,0:T(1,128)S(1)}, f32[1,768]{1,0:T(1,128)S(1)}, u32[]{:S(2)}, u32[]{:S(2)}) collective-permute-start(f32[1,768]{1,0:T(1,128)S(1)} %get-tuple-element.930), channel_id=1, source_target_pairs={{32,0},{64,32},{96,64},{128,96},{160,128},{192,160},{224,192},{256... | collective-permute-start | bytes 9224 | tf_op jit(solution)/shard_map/ppermute | solution.py:22
  165.2 4.8 collective-permute-start.28
  171.9 3.2 collective-permute-start.14
  177.0 2.6 collective-permute-done.15
  185.1 4.3 collective-permute-start.16
  190.7 3.0 collective-permute-done.17
  195.1 2.6 scatter.206
  199.0 15.4 %scatter.209 = f32[3,2,1,4,8,8,8]{6,5,4,3,1,0,2:T(8,128)S(1)} dynamic-update-slice(f32[3,2,1,4,8,8,8]{6,5,4,3,1,0,2:T(8,128)S(1)} %scatter.206, f32[3,2,1,4,8,8,1]{6,5,4,3,1,0,2:T(8,128)S(1)} %copy.220, s32[]{:T(128)} %constant.1319.clone.1, s32[]{:T(128)} %constant.1319.clone.1, s32[]{:T(128)} %constant.1319.clone.1, s32[]{:T(128)} %constant.1319.clone.1, s32[]{:T(128)} %constant.1319.clone.1, ...) | dynamic-update-slice | bytes 12292 | tf_op jit(solution)/shard_map/scatter | solution.py:63
  219.2 12.8 %collective-permute-start.19 = (f32[1,256]{1,0:T(1,128)S(1)}, f32[1,256]{1,0:T(1,128)S(1)}, u32[]{:S(2)}, u32[]{:S(2)}) collective-permute-start(f32[1,256]{1,0:T(1,128)S(1)} %get-tuple-element.992), channel_id=1, source_target_pairs={{32,0},{64,32},{96,64},{128,96},{160,128},{192,160},{224,192},{256... | collective-permute-start | bytes 3080 | tf_op jit(solution)/shard_map/ppermute | solution.py:22
  236.2 3.0 collective-permute-done.21
  240.3 3.6 collective-permute-start.22
  246.7 4.6 scatter.229
  252.8 4.8 scatter.219
  263.0 11.8 %collective-permute-start.31 = (f32[1,256]{1,0:T(1,128)S(1)}, f32[1,256]{1,0:T(1,128)S(1)}, u32[]{:S(2)}, u32[]{:S(2)}) collective-permute-start(f32[1,256]{1,0:T(1,128)S(1)} %get-tuple-element.986), channel_id=1, source_target_pairs={{32,0},{64,32},{96,64},{128,96},{160,128},{192,160},{224,192},{256... | collective-permute-start | bytes 3080 | tf_op jit(solution)/shard_map/ppermute | solution.py:22
  279.1 3.0 collective-permute-done.33
  283.2 4.3 collective-permute-start.34
  288.8 3.4 collective-permute-done.35
  293.7 4.6 scatter.239
  299.1 107.2 %all-reduce = (f32[]{:T(128)}, f32[]{:T(128)}) all-reduce(f32[]{:T(128)} %get-tuple-element.811, f32[]{:T(128)} %get-tuple-element.810), channel_id=1, replica_groups=mesh['gx'=16,'gy'=4,'gz'=8] {'gx','gy','gz'}, use_global_device_ids=true, to_apply=%region_2.15 | all-reduce | flops 2 | bytes 16 | tf_op jit(solution)/shard_map/psum | solution.py:165
  408.4 94.4 %psum.58 = f32[]{:T(128)} all-reduce(f32[]{:T(128)} %get-tuple-element.862), channel_id=1, replica_groups=mesh['gx'=16,'gy'=4,'gz'=8] {'gx','gy','gz'}, use_global_device_ids=true, to_apply=%region_6.19 | all-reduce | flops 1 | bytes 8 | tf_op jit(solution)/shard_map/psum | solution.py:165
  507.7 4.2 collective-permute-start.36
  513.9 3.2 collective-permute-done.37
  517.5 3.9 collective-permute-start.38
  522.8 3.0 collective-permute-done.39
  530.3 3.7 collective-permute-done.41
  535.5 4.6 scatter.249
  540.9 104.3 %psum.59 = f32[]{:T(128)} all-reduce(f32[]{:T(128)} %fusion.31), channel_id=1, replica_groups=mesh['gx'=16,'gy'=4,'gz'=8] {'gx','gy','gz'}, use_global_device_ids=true, to_apply=%region_8.21 | all-reduce | flops 1 | bytes 8 | tf_op jit(solution)/shard_map/psum | solution.py:182
  647.9 94.4 %psum.60 = f32[]{:T(128)} all-reduce(f32[]{:T(128)} %get-tuple-element.859), channel_id=1, replica_groups=mesh['gx'=16,'gy'=4,'gz'=8] {'gx','gy','gz'}, use_global_device_ids=true, to_apply=%region_10.23 | all-reduce | flops 1 | bytes 8 | tf_op jit(solution)/shard_map/psum | solution.py:165
  747.1 4.2 collective-permute-start.42
  753.3 3.2 collective-permute-done.43
  757.0 2.7 collective-permute-start.44
  761.1 3.0 collective-permute-done.45
  765.2 2.2 collective-permute-start.46
  768.7 3.9 collective-permute-done.47
  774.1 4.6 scatter.259
  779.5 103.8 %psum.61 = f32[]{:T(128)} all-reduce(f32[]{:T(128)} %fusion.33), channel_id=1, replica_groups=mesh['gx'=16,'gy'=4,'gz'=8] {'gx','gy','gz'}, use_global_device_ids=true, to_apply=%region_12.25 | all-reduce | flops 1 | bytes 8 | tf_op jit(solution)/shard_map/psum | solution.py:182
  886.0 94.7 %psum.62 = f32[]{:T(128)} all-reduce(f32[]{:T(128)} %get-tuple-element.856), channel_id=1, replica_groups=mesh['gx'=16,'gy'=4,'gz'=8] {'gx','gy','gz'}, use_global_device_ids=true, to_apply=%region_14.27 | all-reduce | flops 1 | bytes 8 | tf_op jit(solution)/shard_map/psum | solution.py:165
  985.5 4.2 collective-permute-start.48
  991.7 3.2 collective-permute-done.49
  995.3 2.8 collective-permute-start.50
  999.5 3.0 collective-permute-done.51
  1003.6 2.2 collective-permute-start.52
  1007.1 3.9 collective-permute-done.53
  1012.5 4.6 scatter.269
  1018.9 103.9 %psum.63 = f32[]{:T(128)} all-reduce(f32[]{:T(128)} %fusion.35), channel_id=1, replica_groups=mesh['gx'=16,'gy'=4,'gz'=8] {'gx','gy','gz'}, use_global_device_ids=true, to_apply=%region_16.29 | all-reduce | flops 1 | bytes 8 | tf_op jit(solution)/shard_map/psum | solution.py:182
  (531 shorter events, 132.6 us)
Async XLA Ops:
  1.9 10.9 copy-start.5
  2.1 27.2 %collective-permute-start = (f32[1,768]{1,0:T(1,128)S(1)}, f32[1,768]{1,0:T(1,128)S(1)}, u32[]{:S(2)}, u32[]{:S(2)}) collective-permute-start(f32[1,768]{1,0:T(1,128)S(1)} %get-tuple-element.945), channel_id=1, source_target_pairs={{0,32},{32,64},{64,96},{96,128},{128,160},{160,192},{192,224},{224... | collective-permute-start | bytes 9224 | tf_op jit(solution)/shard_map/ppermute | solution.py:19
  6.6 22.7 %collective-permute-start.1 = (f32[1,768]{1,0:T(1,128)S(1)}, f32[1,768]{1,0:T(1,128)S(1)}, u32[]{:S(2)}, u32[]{:S(2)}) collective-permute-start(f32[1,768]{1,0:T(1,128)S(1)} %get-tuple-element.946), channel_id=1, source_target_pairs={{32,0},{64,32},{96,64},{128,96},{160,128},{192,160},{224,192},{256... | collective-permute-start | bytes 9224 | tf_op jit(solution)/shard_map/ppermute | solution.py:22
  12.8 0.7 copy-start.6
  12.9 0.7 copy-start.7
  13.9 12.1 %collective-permute-start.24 = (f32[1,256]{1,0:T(1,128)S(1)}, f32[1,256]{1,0:T(1,128)S(1)}, u32[]{:S(2)}, u32[]{:S(2)}) collective-permute-start(f32[1,256]{1,0:T(1,128)S(1)} %get-tuple-element.997), channel_id=1, source_target_pairs={{0,32},{32,64},{64,96},{96,128},{128,160},{160,192},{192,224},{224... | collective-permute-start | bytes 3080 | tf_op jit(solution)/shard_map/ppermute | solution.py:19
  15.8 10.5 collective-permute-start.25
  26.7 8.7 collective-permute-start.26
  28.1 7.3 collective-permute-start.27
  30.0 5.5 collective-permute-start.2
  34.1 4.4 collective-permute-start.3
  44.0 2.6 collective-permute-start.4
  45.3 4.3 collective-permute-start.5
  71.4 0.9 copy-start
  76.0 0.7 copy-start.4
  79.4 15.9 %collective-permute-start.6 = (f32[1,768]{1,0:T(1,128)S(1)}, f32[1,768]{1,0:T(1,128)S(1)}, u32[]{:S(2)}, u32[]{:S(2)}) collective-permute-start(f32[1,768]{1,0:T(1,128)S(1)} %get-tuple-element.937), channel_id=1, source_target_pairs={{0,32},{32,64},{64,96},{96,128},{128,160},{160,192},{192,224},{224... | collective-permute-start | bytes 9224 | tf_op jit(solution)/shard_map/ppermute | solution.py:19
  81.6 13.7 %collective-permute-start.7 = (f32[1,768]{1,0:T(1,128)S(1)}, f32[1,768]{1,0:T(1,128)S(1)}, u32[]{:S(2)}, u32[]{:S(2)}) collective-permute-start(f32[1,768]{1,0:T(1,128)S(1)} %get-tuple-element.938), channel_id=1, source_target_pairs={{32,0},{64,32},{96,64},{128,96},{160,128},{192,160},{224,192},{256... | collective-permute-start | bytes 9224 | tf_op jit(solution)/shard_map/ppermute | solution.py:22
  95.9 4.9 collective-permute-start.8
  99.2 4.4 collective-permute-start.9
  109.1 5.4 collective-permute-start.10
  113.1 6.2 collective-permute-start.11
  150.5 20.8 %collective-permute-start.12 = (f32[1,768]{1,0:T(1,128)S(1)}, f32[1,768]{1,0:T(1,128)S(1)}, u32[]{:S(2)}, u32[]{:S(2)}) collective-permute-start(f32[1,768]{1,0:T(1,128)S(1)} %get-tuple-element.929), channel_id=1, source_target_pairs={{0,32},{32,64},{64,96},{96,128},{128,160},{160,192},{192,224},{224... | collective-permute-start | bytes 9224 | tf_op jit(solution)/shard_map/ppermute | solution.py:19
  152.4 18.9 %collective-permute-start.13 = (f32[1,768]{1,0:T(1,128)S(1)}, f32[1,768]{1,0:T(1,128)S(1)}, u32[]{:S(2)}, u32[]{:S(2)}) collective-permute-start(f32[1,768]{1,0:T(1,128)S(1)} %get-tuple-element.930), channel_id=1, source_target_pairs={{32,0},{64,32},{96,64},{128,96},{160,128},{192,160},{224,192},{256... | collective-permute-start | bytes 9224 | tf_op jit(solution)/shard_map/ppermute | solution.py:22
  165.2 11.8 %collective-permute-start.28 = (f32[1,128]{1,0:T(1,128)S(1)}, f32[1,128]{1,0:T(1,128)S(1)}, u32[]{:S(2)}, u32[]{:S(2)}) collective-permute-start(f32[1,128]{1,0:T(1,128)S(1)} %get-tuple-element.995), channel_id=1, source_target_pairs={{0,1},{1,2},{2,3},{3,4},{4,5},{5,6},{6,7},{8,9},{9,10},{10,11},{11... | collective-permute-start | bytes 1544 | tf_op jit(solution)/shard_map/ppermute | solution.py:19
  170.0 7.0 collective-permute-start.29
  171.9 5.1 collective-permute-start.14
  175.2 4.4 collective-permute-start.15
  185.1 5.6 collective-permute-start.16
  189.4 4.3 collective-permute-start.17
  216.0 0.7 copy-start.3
  217.2 14.7 %collective-permute-start.18 = (f32[1,256]{1,0:T(1,128)S(1)}, f32[1,256]{1,0:T(1,128)S(1)}, u32[]{:S(2)}, u32[]{:S(2)}) collective-permute-start(f32[1,256]{1,0:T(1,128)S(1)} %get-tuple-element.991), channel_id=1, source_target_pairs={{0,32},{32,64},{64,96},{96,128},{128,160},{160,192},{192,224},{224... | collective-permute-start | bytes 3080 | tf_op jit(solution)/shard_map/ppermute | solution.py:19
  219.2 13.6 %collective-permute-start.19 = (f32[1,256]{1,0:T(1,128)S(1)}, f32[1,256]{1,0:T(1,128)S(1)}, u32[]{:S(2)}, u32[]{:S(2)}) collective-permute-start(f32[1,256]{1,0:T(1,128)S(1)} %get-tuple-element.992), channel_id=1, source_target_pairs={{32,0},{64,32},{96,64},{128,96},{160,128},{192,160},{224,192},{256... | collective-permute-start | bytes 3080 | tf_op jit(solution)/shard_map/ppermute | solution.py:22
  233.2 3.1 collective-permute-start.20
  234.9 4.3 collective-permute-start.21
  240.3 11.0 collective-permute-start.22
  243.9 7.4 collective-permute-start.23
  261.1 13.8 %collective-permute-start.30 = (f32[1,256]{1,0:T(1,128)S(1)}, f32[1,256]{1,0:T(1,128)S(1)}, u32[]{:S(2)}, u32[]{:S(2)}) collective-permute-start(f32[1,256]{1,0:T(1,128)S(1)} %get-tuple-element.985), channel_id=1, source_target_pairs={{0,32},{32,64},{64,96},{96,128},{128,160},{160,192},{192,224},{224... | collective-permute-start | bytes 3080 | tf_op jit(solution)/shard_map/ppermute | solution.py:19
  263.0 12.7 %collective-permute-start.31 = (f32[1,256]{1,0:T(1,128)S(1)}, f32[1,256]{1,0:T(1,128)S(1)}, u32[]{:S(2)}, u32[]{:S(2)}) collective-permute-start(f32[1,256]{1,0:T(1,128)S(1)} %get-tuple-element.986), channel_id=1, source_target_pairs={{32,0},{64,32},{96,64},{128,96},{160,128},{192,160},{224,192},{256... | collective-permute-start | bytes 3080 | tf_op jit(solution)/shard_map/ppermute | solution.py:22
  276.1 3.0 collective-permute-start.32
  277.8 4.3 collective-permute-start.33
  283.2 5.6 collective-permute-start.34
  287.5 4.7 collective-permute-start.35
  507.7 6.2 collective-permute-start.36
  511.9 5.2 collective-permute-start.37
  517.5 5.3 collective-permute-start.38
  521.5 4.3 collective-permute-start.39
  527.1 3.2 collective-permute-start.40
  529.0 5.0 collective-permute-start.41
  747.1 6.2 collective-permute-start.42
  751.4 5.2 collective-permute-start.43
  757.0 4.1 collective-permute-start.44
  759.8 4.3 collective-permute-start.45
  765.2 3.5 collective-permute-start.46
  767.4 5.2 collective-permute-start.47
  778.8 105.9 %copy-start.2 = (f32[1,2,1,4,8,8,8]{6,5,4,3,1,2,0:T(8,128)S(1)}, f32[1,2,1,4,8,8,8]{6,5,4,3,1,2,0:T(8,128)}, u32[]{:S(2)}) copy-start(f32[1,2,1,4,8,8,8]{6,5,4,3,1,2,0:T(8,128)} %get-tuple-element.861) | copy-start | bytes 49156
  985.5 6.2 collective-permute-start.48
  989.7 5.2 collective-permute-start.49
  995.3 4.2 collective-permute-start.50
  998.2 4.3 collective-permute-start.51
  1003.6 3.5 collective-permute-start.52
  1005.8 5.2 collective-permute-start.53
  1124.1 1.0 copy-start.1
where the time goes:
time: 1140 us; the launch traced here: 1130 us
  blocking collectives  703 us (62%)
  starting transfers between devices  176 us (15%)
  local copies, waits for them, and re-layouts  148 us (13%)
  waiting for transfers between devices  60.7 us (5%)
  matrix products  17.8 us (2%)
  between operations  13.6 us (1%)
    psum x4, blocking collectives, norm_weighted_mass(): return lax.psum(local_inner(residual_vec, precond_vec), ('gx', 'gy', 'gz'))  391 us
    psum x3, blocking collectives, body(): lax.psum(local_inner(search, applied), ('gx', 'gy', 'gz'))  312 us
    scatter x54, local copies, waits for them, and re-layouts, place_face(): return values.at[selector].set(update)  98.6 us
    ppermute x27, starting transfers between devices, extended(): lax.ppermute(lax.slice_in_dim(block, 0, width, axis=dim), axis, backward)  95.5 us
    ppermute x27, starting transfers between devices, extended(): lax.ppermute(lax.slice_in_dim(block, block.shape[dim] - width, None, axis...  80.1 us
    ppermute x27, waiting for transfers between devices, extended(): lax.ppermute(lax.slice_in_dim(block, 0, width, axis=dim), axis, backward)  60.7 us
  transfers between devices with their start and end apart: 54, of which 21 were waited for; matrix products, arithmetic and copies ran while one was open for 1% of the time, Pallas kernels for 0%

commit v1 on v0

--- a/solution.py
+++ b/solution.py
@@ -179,7 +179,9 @@
                 True,
             )
         applied = assemble(local_sum)
-        step_length = progress / lax.psum(local_inner(search, applied), ("gx", "gy", "gz"))
+        step_length = progress / lax.psum(
+            lax.psum(local_inner(search, applied), ("gy", "gz")), "gx"
+        )
         pressure = pressure + step_length * search
         residual = residual - step_length * applied
         precond = residual / diagonal

time: 1140 us -> 1310 us (1.15)
  blocking collectives: 703 us -> 883 us
    psum x3 -> x8, blocking collectives: 312 us -> 508 us  [the longest x4 259 us: body(): lax.psum(lax.psum(local_inner(search, applied), ('gy', 'gz')), 'gx')]
    psum x4, blocking collectives: 391 us -> 375 us  [norm_weighted_mass(): return lax.psum(local_inner(residual_vec, precond_vec), ('gx', 'gy', 'gz'))]
where the time goes in v1:
time: 1310 us; the launch traced here: 1300 us
  blocking collectives  883 us (67%)
  starting transfers between devices  173 us (13%)
  local copies, waits for them, and re-layouts  148 us (11%)
  waiting for transfers between devices  58 us (4%)
  matrix products  17.9 us (1%)
  between operations  13.6 us (1%)
    psum x4, blocking collectives, norm_weighted_mass(): return lax.psum(local_inner(residual_vec, precond_vec), ('gx', 'gy', 'gz'))  375 us
    psum x4, blocking collectives, body(): lax.psum(lax.psum(local_inner(search, applied), ('gy', 'gz')), 'gx')  259 us
    psum x4, blocking collectives, body(): lax.psum(local_inner(search, applied), ('gy', 'gz'))  249 us
    scatter x54, local copies, waits for them, and re-layouts, place_face(): return values.at[selector].set(update)  98.5 us
    ppermute x27, starting transfers between devices, extended(): lax.ppermute(lax.slice_in_dim(block, 0, width, axis=dim), axis, backward)  95.7 us
    ppermute x27, starting transfers between devices, extended(): lax.ppermute(lax.slice_in_dim(block, block.shape[dim] - width, None, axis...  77.4 us
    ppermute x27, waiting for transfers between devices, extended(): lax.ppermute(lax.slice_in_dim(block, 0, width, axis=dim), axis, backward)  57.9 us
  transfers between devices with their start and end apart: 54, of which 21 were waited for; matrix products, arithmetic and copies ran while one was open for 1% of the time, Pallas kernels for 0%

profile of v1, /device:TPU:1, one launch (start us, length us, event | category | flops | bytes accessed | tf_op | source)
XLA Modules:
  0.0 1302.4 jit_solution(16557383342931311009)
XLA Ops:
  2.1 4.5 collective-permute-start
  6.6 6.2 collective-permute-start.1
  15.8 9.7 collective-permute-start.25
  30.0 4.0 collective-permute-start.2
  35.4 3.0 collective-permute-done.3
  46.6 3.0 collective-permute-done.5
  51.0 2.6 scatter.186
  54.8 15.4 %scatter.189 = f32[3,2,1,4,8,8,8]{6,5,4,3,1,0,2:T(8,128)S(1)} dynamic-update-slice(f32[3,2,1,4,8,8,8]{6,5,4,3,1,0,2:T(8,128)S(1)} %scatter.186, f32[3,2,1,4,8,8,1]{6,5,4,3,1,0,2:T(8,128)S(1)} %copy.186, s32[]{:T(128)} %constant.1319.clone.1, s32[]{:T(128)} %constant.1319.clone.1, s32[]{:T(128)} %constant.1319.clone.1, s32[]{:T(128)} %constant.1319.clone.1, s32[]{:T(128)} %constant.1319.clone.1, ...) | dynamic-update-slice | bytes 12292 | tf_op jit(solution)/shard_map/scatter | solution.py:63
  76.8 2.4 fusion.2
  81.7 12.9 collective-permute-start.7
  95.9 3.2 collective-permute-start.8
  100.9 2.8 collective-permute-done.9
  109.2 4.0 collective-permute-start.10
  114.6 4.7 collective-permute-done.11
  122.2 2.6 scatter.196
  127.6 15.4 %scatter.199 = f32[3,2,1,4,8,8,8]{6,5,4,3,1,0,2:T(8,128)S(1)} dynamic-update-slice(f32[3,2,1,4,8,8,8]{6,5,4,3,1,0,2:T(8,128)S(1)} %scatter.196, f32[3,2,1,4,8,8,1]{6,5,4,3,1,0,2:T(8,128)S(1)} %copy.203, s32[]{:T(128)} %constant.1319.clone.1, s32[]{:T(128)} %constant.1319.clone.1, s32[]{:T(128)} %constant.1319.clone.1, s32[]{:T(128)} %constant.1319.clone.1, s32[]{:T(128)} %constant.1319.clone.1, ...) | dynamic-update-slice | bytes 12292 | tf_op jit(solution)/shard_map/scatter | solution.py:63
  152.5 12.7 collective-permute-start.13
  165.2 4.8 collective-permute-start.28
  172.0 3.2 collective-permute-start.14
  177.0 2.6 collective-permute-done.15
  185.2 4.3 collective-permute-start.16
  190.8 3.0 collective-permute-done.17
  195.1 2.6 scatter.206
  199.0 15.4 %scatter.209 = f32[3,2,1,4,8,8,8]{6,5,4,3,1,0,2:T(8,128)S(1)} dynamic-update-slice(f32[3,2,1,4,8,8,8]{6,5,4,3,1,0,2:T(8,128)S(1)} %scatter.206, f32[3,2,1,4,8,8,1]{6,5,4,3,1,0,2:T(8,128)S(1)} %copy.220, s32[]{:T(128)} %constant.1319.clone.1, s32[]{:T(128)} %constant.1319.clone.1, s32[]{:T(128)} %constant.1319.clone.1, s32[]{:T(128)} %constant.1319.clone.1, s32[]{:T(128)} %constant.1319.clone.1, ...) | dynamic-update-slice | bytes 12292 | tf_op jit(solution)/shard_map/scatter | solution.py:63
  219.2 12.8 collective-permute-start.19
  236.2 3.0 collective-permute-done.21
  240.3 3.6 collective-permute-start.22
  246.7 4.6 scatter.229
  252.8 4.8 scatter.219
  263.0 11.8 collective-permute-start.31
  279.2 3.0 collective-permute-done.33
  283.2 4.3 collective-permute-start.34
  288.8 3.4 collective-permute-done.35
  293.7 4.6 scatter.239
  299.1 63.1 %psum.85 = f32[]{:T(128)} all-reduce(f32[]{:T(128)} %get-tuple-element.810), channel_id=1, replica_groups=mesh['gx'=16,'gy'=4,'gz'=8] {'gy','gz'}, use_global_device_ids=true, to_apply=%region_4.17 | all-reduce | flops 1 | bytes 8 | tf_op jit(solution)/shard_map/psum | solution.py:183
  362.2 67.4 %psum.86 = f32[]{:T(128)} all-reduce(f32[]{:T(128)} %psum.85), channel_id=1, replica_groups=mesh['gx'=16,'gy'=4,'gz'=8] {'gx'}, use_global_device_ids=true, to_apply=%region_5.18 | all-reduce | flops 1 | bytes 8 | tf_op jit(solution)/shard_map/psum | solution.py:182
  429.6 93.5 %psum.84 = f32[]{:T(128)} all-reduce(f32[]{:T(128)} %get-tuple-element.811), channel_id=1, replica_groups=mesh['gx'=16,'gy'=4,'gz'=8] {'gx','gy','gz'}, use_global_device_ids=true, to_apply=%region_2.15 | all-reduce | flops 1 | bytes 8 | tf_op jit(solution)/shard_map/psum | solution.py:165
  525.2 94.4 %psum.87 = f32[]{:T(128)} all-reduce(f32[]{:T(128)} %get-tuple-element.860), channel_id=1, replica_groups=mesh['gx'=16,'gy'=4,'gz'=8] {'gx','gy','gz'}, use_global_device_ids=true, to_apply=%region_7.20 | all-reduce | flops 1 | bytes 8 | tf_op jit(solution)/shard_map/psum | solution.py:165
  624.4 3.4 collective-permute-start.36
  629.8 3.2 collective-permute-done.37
  633.4 3.6 collective-permute-start.38
  638.6 2.8 collective-permute-done.39
  642.5 2.3 collective-permute-start.40
  646.1 3.0 collective-permute-done.41
  650.5 4.6 scatter.249
  655.9 61.5 %psum.88 = f32[]{:T(128)} all-reduce(f32[]{:T(128)} %fusion.31), channel_id=1, replica_groups=mesh['gx'=16,'gy'=4,'gz'=8] {'gy','gz'}, use_global_device_ids=true, to_apply=%region_9.22 | all-reduce | flops 1 | bytes 8 | tf_op jit(solution)/shard_map/psum | solution.py:183
  717.4 64.6 %psum.89 = f32[]{:T(128)} all-reduce(f32[]{:T(128)} %psum.88), channel_id=1, replica_groups=mesh['gx'=16,'gy'=4,'gz'=8] {'gx'}, use_global_device_ids=true, to_apply=%region_10.23 | all-reduce | flops 1 | bytes 8 | tf_op jit(solution)/shard_map/psum | solution.py:182
  784.7 93.5 %psum.90 = f32[]{:T(128)} all-reduce(f32[]{:T(128)} %get-tuple-element.857), channel_id=1, replica_groups=mesh['gx'=16,'gy'=4,'gz'=8] {'gx','gy','gz'}, use_global_device_ids=true, to_apply=%region_12.25 | all-reduce | flops 1 | bytes 8 | tf_op jit(solution)/shard_map/psum | solution.py:165
  883.0 4.2 collective-permute-start.42
  889.2 3.2 collective-permute-done.43
  896.1 3.0 collective-permute-done.45
  903.3 3.0 collective-permute-done.47
  907.7 4.6 scatter.259
  913.2 62.4 %psum.91 = f32[]{:T(128)} all-reduce(f32[]{:T(128)} %fusion.33), channel_id=1, replica_groups=mesh['gx'=16,'gy'=4,'gz'=8] {'gy','gz'}, use_global_device_ids=true, to_apply=%region_14.27 | all-reduce | flops 1 | bytes 8 | tf_op jit(solution)/shard_map/psum | solution.py:183
  975.5 63.9 %psum.92 = f32[]{:T(128)} all-reduce(f32[]{:T(128)} %psum.91), channel_id=1, replica_groups=mesh['gx'=16,'gy'=4,'gz'=8] {'gx'}, use_global_device_ids=true, to_apply=%region_15.28 | all-reduce | flops 1 | bytes 8 | tf_op jit(solution)/shard_map/psum | solution.py:182
  1042.2 93.8 %psum.93 = f32[]{:T(128)} all-reduce(f32[]{:T(128)} %get-tuple-element.854), channel_id=1, replica_groups=mesh['gx'=16,'gy'=4,'gz'=8] {'gx','gy','gz'}, use_global_device_ids=true, to_apply=%region_17.30 | all-reduce | flops 1 | bytes 8 | tf_op jit(solution)/shard_map/psum | solution.py:165
  1140.7 4.2 collective-permute-start.48
  1146.9 3.2 collective-permute-done.49
  1150.5 2.3 collective-permute-start.50
  1154.2 3.0 collective-permute-done.51
  1161.8 3.0 collective-permute-done.53
  1166.2 4.6 scatter.269
  1171.6 62.4 %psum.94 = f32[]{:T(128)} all-reduce(f32[]{:T(128)} %fusion.35), channel_id=1, replica_groups=mesh['gx'=16,'gy'=4,'gz'=8] {'gy','gz'}, use_global_device_ids=true, to_apply=%region_19.32 | all-reduce | flops 1 | bytes 8 | tf_op jit(solution)/shard_map/psum | solution.py:183
  1235.0 63.1 %psum.95 = f32[]{:T(128)} all-reduce(f32[]{:T(128)} %psum.94), channel_id=1, replica_groups=mesh['gx'=16,'gy'=4,'gz'=8] {'gx'}, use_global_device_ids=true, to_apply=%region_20.33 | all-reduce | flops 1 | bytes 8 | tf_op jit(solution)/shard_map/psum | solution.py:182
  (536 shorter events, 142.9 us)
Async XLA Ops:
  1.9 10.9 copy-start.5
  2.1 27.2 %collective-permute-start = (f32[1,768]{1,0:T(1,128)S(1)}, f32[1,768]{1,0:T(1,128)S(1)}, u32[]{:S(2)}, u32[]{:S(2)}) collective-permute-start(f32[1,768]{1,0:T(1,128)S(1)} %get-tuple-element.943), channel_id=1, source_target_pairs={{0,32},{32,64},{64,96},{96,128},{128,160},{160,192},{192,224},{224... | collective-permute-start | bytes 9224 | tf_op jit(solution)/shard_map/ppermute | solution.py:19
  6.6 22.7 %collective-permute-start.1 = (f32[1,768]{1,0:T(1,128)S(1)}, f32[1,768]{1,0:T(1,128)S(1)}, u32[]{:S(2)}, u32[]{:S(2)}) collective-permute-start(f32[1,768]{1,0:T(1,128)S(1)} %get-tuple-element.944), channel_id=1, source_target_pairs={{32,0},{64,32},{96,64},{128,96},{160,128},{192,160},{224,192},{256... | collective-permute-start | bytes 9224 | tf_op jit(solution)/shard_map/ppermute | solution.py:22
  12.8 0.7 copy-start.6
  12.9 0.7 copy-start.7
  13.9 12.1 collective-permute-start.24
  15.8 10.5 collective-permute-start.25
  26.7 8.7 collective-permute-start.26
  28.1 7.3 collective-permute-start.27
  30.0 5.5 collective-permute-start.2
  34.1 4.4 collective-permute-start.3
  44.0 2.6 collective-permute-start.4
  45.3 4.3 collective-permute-start.5
  71.4 0.9 copy-start
  76.1 0.7 copy-start.4
  79.4 15.9 %collective-permute-start.6 = (f32[1,768]{1,0:T(1,128)S(1)}, f32[1,768]{1,0:T(1,128)S(1)}, u32[]{:S(2)}, u32[]{:S(2)}) collective-permute-start(f32[1,768]{1,0:T(1,128)S(1)} %get-tuple-element.935), channel_id=1, source_target_pairs={{0,32},{32,64},{64,96},{96,128},{128,160},{160,192},{192,224},{224... | collective-permute-start | bytes 9224 | tf_op jit(solution)/shard_map/ppermute | solution.py:19
  81.7 13.7 %collective-permute-start.7 = (f32[1,768]{1,0:T(1,128)S(1)}, f32[1,768]{1,0:T(1,128)S(1)}, u32[]{:S(2)}, u32[]{:S(2)}) collective-permute-start(f32[1,768]{1,0:T(1,128)S(1)} %get-tuple-element.936), channel_id=1, source_target_pairs={{32,0},{64,32},{96,64},{128,96},{160,128},{192,160},{224,192},{256... | collective-permute-start | bytes 9224 | tf_op jit(solution)/shard_map/ppermute | solution.py:22
  95.9 4.9 collective-permute-start.8
  99.3 4.4 collective-permute-start.9
  109.2 5.4 collective-permute-start.10
  113.2 6.2 collective-permute-start.11
  150.5 20.8 %collective-permute-start.12 = (f32[1,768]{1,0:T(1,128)S(1)}, f32[1,768]{1,0:T(1,128)S(1)}, u32[]{:S(2)}, u32[]{:S(2)}) collective-permute-start(f32[1,768]{1,0:T(1,128)S(1)} %get-tuple-element.927), channel_id=1, source_target_pairs={{0,32},{32,64},{64,96},{96,128},{128,160},{160,192},{192,224},{224... | collective-permute-start | bytes 9224 | tf_op jit(solution)/shard_map/ppermute | solution.py:19
  152.5 18.9 %collective-permute-start.13 = (f32[1,768]{1,0:T(1,128)S(1)}, f32[1,768]{1,0:T(1,128)S(1)}, u32[]{:S(2)}, u32[]{:S(2)}) collective-permute-start(f32[1,768]{1,0:T(1,128)S(1)} %get-tuple-element.928), channel_id=1, source_target_pairs={{32,0},{64,32},{96,64},{128,96},{160,128},{192,160},{224,192},{256... | collective-permute-start | bytes 9224 | tf_op jit(solution)/shard_map/ppermute | solution.py:22
  165.2 11.8 collective-permute-start.28
  170.1 6.9 collective-permute-start.29
  172.0 5.1 collective-permute-start.14
  175.3 4.4 collective-permute-start.15
  185.2 5.6 collective-permute-start.16
  189.4 4.3 collective-permute-start.17
  216.0 0.7 copy-start.3
  217.2 14.7 %collective-permute-start.18 = (f32[1,256]{1,0:T(1,128)S(1)}, f32[1,256]{1,0:T(1,128)S(1)}, u32[]{:S(2)}, u32[]{:S(2)}) collective-permute-start(f32[1,256]{1,0:T(1,128)S(1)} %get-tuple-element.989), channel_id=1, source_target_pairs={{0,32},{32,64},{64,96},{96,128},{128,160},{160,192},{192,224},{224... | collective-permute-start | bytes 3080 | tf_op jit(solution)/shard_map/ppermute | solution.py:19
  219.2 13.6 %collective-permute-start.19 = (f32[1,256]{1,0:T(1,128)S(1)}, f32[1,256]{1,0:T(1,128)S(1)}, u32[]{:S(2)}, u32[]{:S(2)}) collective-permute-start(f32[1,256]{1,0:T(1,128)S(1)} %get-tuple-element.990), channel_id=1, source_target_pairs={{32,0},{64,32},{96,64},{128,96},{160,128},{192,160},{224,192},{256... | collective-permute-start | bytes 3080 | tf_op jit(solution)/shard_map/ppermute | solution.py:22
  233.2 3.0 collective-permute-start.20
  234.9 4.3 collective-permute-start.21
  240.3 11.0 collective-permute-start.22
  243.9 7.4 collective-permute-start.23
  261.1 13.8 %collective-permute-start.30 = (f32[1,256]{1,0:T(1,128)S(1)}, f32[1,256]{1,0:T(1,128)S(1)}, u32[]{:S(2)}, u32[]{:S(2)}) collective-permute-start(f32[1,256]{1,0:T(1,128)S(1)} %get-tuple-element.983), channel_id=1, source_target_pairs={{0,32},{32,64},{64,96},{96,128},{128,160},{160,192},{192,224},{224... | collective-permute-start | bytes 3080 | tf_op jit(solution)/shard_map/ppermute | solution.py:19
  263.0 12.7 collective-permute-start.31
  276.1 3.0 collective-permute-start.32
  277.8 4.3 collective-permute-start.33
  283.2 5.6 collective-permute-start.34
  287.5 4.7 collective-permute-start.35
  624.4 5.3 collective-permute-start.36
  627.8 5.2 collective-permute-start.37
  633.4 5.2 collective-permute-start.38
  637.1 4.3 collective-permute-start.39
  642.5 3.6 collective-permute-start.40
  644.8 4.3 collective-permute-start.41
  883.0 6.2 collective-permute-start.42
  887.3 5.2 collective-permute-start.43
  892.9 3.3 collective-permute-start.44
  894.8 4.3 collective-permute-start.45
  900.2 3.1 collective-permute-start.46
  902.0 4.3 collective-permute-start.47
  912.4 128.4 %copy-start.2 = (f32[1,2,1,4,8,8,8]{6,5,4,3,1,2,0:T(8,128)S(1)}, f32[1,2,1,4,8,8,8]{6,5,4,3,1,2,0:T(8,128)}, u32[]{:S(2)}) copy-start(f32[1,2,1,4,8,8,8]{6,5,4,3,1,2,0:T(8,128)} %get-tuple-element.859) | copy-start | bytes 49156
  1140.7 6.2 collective-permute-start.48
  1144.9 5.2 collective-permute-start.49
  1150.5 3.7 collective-permute-start.50
  1152.9 4.3 collective-permute-start.51
  1158.3 3.4 collective-permute-start.52
  1160.4 4.3 collective-permute-start.53
  1299.4 1.0 copy-start.1
